TPU v7x, 256 devices: a whole 4x4x8 slice. The times are simulated.
256 devices in a mesh: xy: 32 (over y_hi, z, core), gz: 8 (over y_lo, x).
Axes of the slice: x: 4, y: 4 (y_hi: 2, y_lo: 2; y = y_hi * 2 + y_lo), z: 8, core: 2. Of those that a mesh axis runs over, the one named last changes fastest.
Arguments:
- positions: float32 [3, 32, 6, 32, 128], P(None, 'xy', None, 'gz'), may hold values from 0 to 1
- cotangent: float32 [3, 32, 6, 32, 128], P(None, 'xy', None, 'gz'), may hold values from -6 to 6
- species: int32 [32, 6, 32, 128], P('xy', None, 'gz'), may hold values from 0 to 7
- counts: int32 [32, 6, 32], P('xy', None, 'gz'), may hold values from 8 to 128, as said below
- amplitude: float32 [8, 8], replicated, may hold values from 0.2 to 2
Outputs:
- position_cotangent: float32 [3, 32, 6, 32, 128], P(None, 'xy', None, 'gz')
- amplitude_grad: float32 [8, 8], replicated
Inputs may be any that keep to these rules, and one draw needn't show every extreme that they name: The live beads of a cell fill its first counts slots; cell (0, 0, 0) holds 128 beads.
All inputs are finite; a program needn't handle non-finite values.
Results may differ from a plain program's by a relative error of at most 0.00021.
Values sent between devices are 32-bit elements; how exact they have to be, the bound alone decides.
No kernel may reach another device: no remote copies, remote signals or barrier semaphores. Data moves between devices by JAX's collectives and lax.ppermute only.
A program may use at most 64 MiB of HBM per device.

v0:
```python
import functools
import math

import jax
import jax.numpy as jnp
import numpy as np
from jax import lax
from jax.sharding import Mesh
from jax.sharding import PartitionSpec as P

GZ = ("gz_0", "gz_1")
XY = ("xy_0", "xy_1", "xy_2")
XY_GZ = ("xy_0", "xy_1", "xy_2", "gz_0", "gz_1")


HIGHEST = lax.Precision.HIGHEST
step_size = 0.05
half_shell = np.array(
    [[1, dy, dz] for dy in (-1, 0, 1) for dz in (-1, 0, 1)]
    + [[0, 1, dz] for dz in (-1, 0, 1)]
    + [[0, 0, 1]],
    np.int32,
)


def padded(block, sides, width):
    for axis, dim in sides:
        count = lax.axis_size(axis)
        forward = [(i, i + 1) for i in range(count - 1)]
        forward.append((count - 1, 0))
        backward = [(target, source) for source, target in forward]
        low = lax.ppermute(
            lax.slice_in_dim(block, block.shape[dim] - width, None, axis=dim), axis, forward
        )
        high = lax.ppermute(lax.slice_in_dim(block, 0, width, axis=dim), axis, backward)
        block = jnp.concatenate([low, block, high], axis=dim)
    return block


def shifted(block, axis, distance):
    devices = range(lax.axis_size(axis))
    route = [((i - distance) % len(devices), i) for i in devices]
    return lax.ppermute(block, axis, route)


def over_axes(array, axes):
    return functools.reduce(lax.psum, axes, array)


def pair_block(
    pos_home,
    grad_home,
    kind_home,
    live_home,
    pos_far,
    grad_far,
    kind_far,
    live_far,
    offset,
    pair_table,
):
    displace = pos_home[:, :, :, None] - pos_far[:, :, None, :] - offset[:, None, None, None]
    square = jnp.sum(displace * displace, axis=0)
    envelope = jnp.maximum(1.0 - square, 0.0) * live_home[:, :, None] * live_far[:, None, :]
    differ = grad_home[:, :, :, None] - grad_far[:, :, None, :]
    projection = jnp.sum(displace * differ, axis=0)
    mixed_row = jnp.einsum("tmb,st->smb", kind_far, pair_table, precision=HIGHEST)
    strength = jnp.einsum("sma,smb->mab", kind_home, mixed_row, precision=HIGHEST)
    response = 6.0 * strength * envelope * (envelope * differ - 4.0 * displace * projection)
    home_part = jnp.sum(response, axis=3)
    away_part = -jnp.sum(response, axis=2)
    weight = 6.0 * envelope * envelope * projection
    weighted = jnp.einsum("sma,mab->smb", kind_home, weight, precision=HIGHEST)
    pair_matrix = jnp.einsum("smb,tmb->st", weighted, kind_far, precision=HIGHEST)
    return (home_part, away_part, pair_matrix)


def unpack(block, kind_count):
    kinds = jnp.arange(kind_count, dtype=jnp.float32)
    onehot = (block[6][None] == kinds[:, None, None]).astype(jnp.float32)
    return (block[0:3], block[3:6], onehot, block[7])


def grouped(home_block, far_block, offset, pair_table):
    channels, cells, width = home_block.shape
    groups = cells // 8
    kind_count = pair_table.shape[0]

    def regroup(block):
        return jnp.moveaxis(block.reshape(channels, groups, 8, width), 1, 0)

    def one_group(items):
        home_item, far_item = items
        return pair_block(
            *unpack(home_item, kind_count), *unpack(far_item, kind_count), offset, pair_table
        )

    home_parts, away_parts, mats = lax.map(one_group, (regroup(home_block), regroup(far_block)))

    def ungroup(part):
        return jnp.moveaxis(part, 0, 1).reshape(3, cells, width)

    return (ungroup(home_parts), ungroup(away_parts), jnp.sum(mats, axis=0))


def sweep(extended, home_start, shifts, pair_table, width, block_shape):
    cells_x, cells_y, cells_z = block_shape
    channels = extended.shape[0]
    home_block = extended[
        :, home_start : home_start + cells_x, 1 : 1 + cells_y, 1 : 1 + cells_z
    ].reshape(channels, -1, width)
    cells = home_block.shape[1]
    away_shape = (3,) + extended.shape[1:]
    kind_count = pair_table.shape[0]

    def advance(carry, shift):
        home_sum, away_sum, matrix = carry
        start = (0, home_start + shift[0], 1 + shift[1], 1 + shift[2], 0)
        far_block = lax.dynamic_slice(
            extended, start, (channels, cells_x, cells_y, cells_z, width)
        ).reshape(channels, cells, width)
        home_part, away_part, pair_matrix = grouped(
            home_block, far_block, shift.astype(jnp.float32), pair_table
        )
        region = lax.dynamic_slice(away_sum, start, (3, cells_x, cells_y, cells_z, width))
        away_sum = lax.dynamic_update_slice(
            away_sum, region + away_part.reshape(3, cells_x, cells_y, cells_z, width), start
        )
        return ((home_sum + home_part, away_sum, matrix + pair_matrix), None)

    initial = (
        jnp.zeros((3, cells, width), jnp.float32),
        jnp.zeros(away_shape, jnp.float32),
        jnp.zeros((kind_count, kind_count), jnp.float32),
    )
    (home_sum, away_sum, matrix), unused = lax.scan(advance, initial, jnp.asarray(shifts))
    return (home_sum, away_sum, matrix, home_block)


def wrap_y(field):
    return jnp.concatenate([field[:, :, -1:], field, field[:, :, :1]], axis=2)


def per_device(positions, cotangent, species, counts, amplitude):
    slot_count = positions.shape[-1]
    cells_x, cells_y, cells_z = (positions.shape[1], positions.shape[2], positions.shape[3])
    block_shape = (cells_x, cells_y, cells_z)
    pair_table = 0.5 * (amplitude + amplitude.T)
    slots = jnp.arange(slot_count, dtype=jnp.int32)
    live = (slots < counts[..., None]).astype(jnp.float32)
    packed = jnp.concatenate(
        [positions, cotangent, species[None].astype(jnp.float32), live[None]], axis=0
    )
    zpadded = padded(packed, ((GZ, 3),), 1)
    ghost = shifted(zpadded, XY, -1)
    extended = wrap_y(jnp.concatenate([zpadded, ghost], axis=1))
    home_sum, away_sum, matrix, home_block = sweep(
        extended, 0, half_shell, pair_table, slot_count, block_shape
    )
    self_home, unused, self_matrix = grouped(
        home_block, home_block, jnp.zeros((3,), jnp.float32), pair_table
    )
    home_total = home_sum + self_home
    local_matrix = self_matrix + matrix + matrix.T
    folded = away_sum[:, :, 1 : cells_y + 1]
    folded = folded.at[:, :, 0].add(away_sum[:, :, cells_y + 1])
    folded = folded.at[:, :, cells_y - 1].add(away_sum[:, :, 0])
    returned = shifted(folded[:, cells_x : cells_x + 1], XY, 1)
    owned = folded[:, :cells_x].at[:, 0:1].add(returned)
    upper = shifted(owned[:, :, :, cells_z + 1 : cells_z + 2], GZ, 1)
    lower = shifted(owned[:, :, :, 0:1], GZ, -1)
    inner = owned[:, :, :, 1 : cells_z + 1]
    inner = inner.at[:, :, :, 0:1].add(upper)
    inner = inner.at[:, :, :, cells_z - 1 : cells_z].add(lower)
    total = home_total.reshape(3, cells_x, cells_y, cells_z, slot_count) + inner
    position_cotangent = cotangent + step_size * total
    cells_total = cells_x * lax.axis_size(XY) * cells_y * cells_z * lax.axis_size(GZ)
    summed = over_axes(local_matrix, XY_GZ)
    amplitude_grad = step_size * summed / (2.0 * math.sqrt(cells_total / slot_count))
    return (position_cotangent, amplitude_grad)


def solution(mesh):
    finer = Mesh(mesh.devices.reshape(2, 8, 2, 2, 4), ("xy_0", "xy_1", "xy_2", "gz_0", "gz_1"))
    in_specs = (
        P(None, XY, None, GZ, None),
        P(None, XY, None, GZ, None),
        P(XY, None, GZ, None),
        P(XY, None, GZ),
        P(),
    )
    out_specs = (P(None, XY, None, GZ, None), P())
    return jax.shard_map(
        per_device, mesh=finer, in_specs=in_specs, out_specs=out_specs, check_vma=False
    )
```

profile of v0, /device:TPU:1, one launch (start us, length us, event | category | flops | bytes accessed | tf_op | source)
XLA Modules:
  0.0 322.4 jit_solution(6489233279791678025)
XLA Ops:
  3.9 2.1 collective-permute-start
  6.0 2.4 collective-permute-start.1
  9.6 3.7 %collective-permute-start.2 = (f32[8,1,6,6,128]{4,0,3,2,1:T(8,128)S(1)}, f32[8,1,6,6,128]{4,0,3,2,1:T(8,128)S(1)}, u32[]{:S(2)}, u32[]{:S(2)}) collective-permute-start(f32[8,1,6,6,128]{4,0,3,2,1:T(8,128)S(1)} %pad_maximum_fusion.12), channel_id=1, source_target_pairs={{8,0},{16,8},{24,16},{32,24},{40,32},{48,40},{56,48},{64,56},{72,6... | collective-permute-start | bytes 442376 | tf_op jit(solution)/shard_map/ppermute | solution.py:43
  13.3 12.4 %while.69 = (s32[]{:T(128)}, f32[3,3,8,128]{3,2,1,0:T(8,128)S(1)}, f32[3,8,8]{2,1,0:T(8,128)S(1)}, f32[3,8,8,128]{3,2,0,1:T(8,128)S(1)}, f32[8,8]{1,0:T(8,128)S(1)}, /*index=5*/s32[]{:T(128)}) while((s32[]{:T(128)}, f32[3,3,8,128]{3,2,1,0:T(8,128)S(1)}, f32[3,8,8]{2,1,0:T(8,128)S(1)}, f32[3,8,8,128]{3,2,0,1:T(8,128)S(1)}, ...), condition=%wide.region_13.14_spmd, body=%wide.region_9.13_spmd.sunk | while | flops 32928768 | bytes 7188825 | solution.py:98
  15.9 1.5 fusion.69
  25.9 249.4 %while.71 = (s32[]{:T(128)}, f32[3,24,128]{2,1,0:T(8,128)S(1)}, f32[3,2,8,6,128]{4,3,2,1,0:T(8,128)S(1)}, f32[8,8]{1,0:T(8,128)S(1)}, f32[8,1,6,4,128]{4,0,3,2,1...) while((s32[]{:T(128)}, f32[3,24,128]{2,1,0:T(8,128)S(1)}, ...), condition=%wide.region_8.9_spmd.clone.clone, body=%wide.region_0.8_spmd.sunk.clone.clone.sunk | while | flops 34136340 | bytes 7944967 | solution.py:136
  31.8 13.0 %while.72 = (s32[]{:T(128)}, f32[3,3,8,128]{3,2,1,0:T(8,128)S(1)}, f32[3,3,8,128]{3,2,1,0:T(8,128)S(1)}, f32[3,8,8]{2,1,0:T(8,128)S(1)}, f32[3,8,8,128]{3,1,2,0:...) while((s32[]{:T(128)}, f32[3,3,8,128]{3,2,1,0:T(8,128)S(1)}, ...), condition=%wide.region_6.6_spmd, body=%wide.region_1.5_spmd.sunk | while | flops 34108420 | bytes 7377393 | solution.py:98
  34.6 1.5 fusion.78
  38.9 1.5 fusion.78
  43.2 1.5 fusion.78
  51.0 13.0 %while.72 = (s32[]{:T(128)}, f32[3,3,8,128]{3,2,1,0:T(8,128)S(1)}, f32[3,3,8,128]{3,2,1,0:T(8,128)S(1)}, f32[3,8,8]{2,1,0:T(8,128)S(1)}, f32[3,8,8,128]{3,1,2,0:...) while((s32[]{:T(128)}, f32[3,3,8,128]{3,2,1,0:T(8,128)S(1)}, ...), condition=%wide.region_6.6_spmd, body=%wide.region_1.5_spmd.sunk | while | flops 34108420 | bytes 7377393 | solution.py:98
  53.8 1.5 fusion.78
  58.1 1.5 fusion.78
  62.4 1.5 fusion.78
  70.1 13.0 %while.72 = (s32[]{:T(128)}, f32[3,3,8,128]{3,2,1,0:T(8,128)S(1)}, f32[3,3,8,128]{3,2,1,0:T(8,128)S(1)}, f32[3,8,8]{2,1,0:T(8,128)S(1)}, f32[3,8,8,128]{3,1,2,0:...) while((s32[]{:T(128)}, f32[3,3,8,128]{3,2,1,0:T(8,128)S(1)}, ...), condition=%wide.region_6.6_spmd, body=%wide.region_1.5_spmd.sunk | while | flops 34108420 | bytes 7377393 | solution.py:98
  72.9 1.5 fusion.78
  77.3 1.5 fusion.78
  81.6 1.5 fusion.78
  89.3 13.0 %while.72 = (s32[]{:T(128)}, f32[3,3,8,128]{3,2,1,0:T(8,128)S(1)}, f32[3,3,8,128]{3,2,1,0:T(8,128)S(1)}, f32[3,8,8]{2,1,0:T(8,128)S(1)}, f32[3,8,8,128]{3,1,2,0:...) while((s32[]{:T(128)}, f32[3,3,8,128]{3,2,1,0:T(8,128)S(1)}, ...), condition=%wide.region_6.6_spmd, body=%wide.region_1.5_spmd.sunk | while | flops 34108420 | bytes 7377393 | solution.py:98
  92.1 1.5 fusion.78
  96.5 1.5 fusion.78
  100.8 1.5 fusion.78
  108.5 13.0 %while.72 = (s32[]{:T(128)}, f32[3,3,8,128]{3,2,1,0:T(8,128)S(1)}, f32[3,3,8,128]{3,2,1,0:T(8,128)S(1)}, f32[3,8,8]{2,1,0:T(8,128)S(1)}, f32[3,8,8,128]{3,1,2,0:...) while((s32[]{:T(128)}, f32[3,3,8,128]{3,2,1,0:T(8,128)S(1)}, ...), condition=%wide.region_6.6_spmd, body=%wide.region_1.5_spmd.sunk | while | flops 34108420 | bytes 7377393 | solution.py:98
  111.3 1.5 fusion.78
  115.6 1.5 fusion.78
  120.0 1.5 fusion.78
  127.7 13.0 %while.72 = (s32[]{:T(128)}, f32[3,3,8,128]{3,2,1,0:T(8,128)S(1)}, f32[3,3,8,128]{3,2,1,0:T(8,128)S(1)}, f32[3,8,8]{2,1,0:T(8,128)S(1)}, f32[3,8,8,128]{3,1,2,0:...) while((s32[]{:T(128)}, f32[3,3,8,128]{3,2,1,0:T(8,128)S(1)}, ...), condition=%wide.region_6.6_spmd, body=%wide.region_1.5_spmd.sunk | while | flops 34108420 | bytes 7377393 | solution.py:98
  130.5 1.5 fusion.78
  134.8 1.5 fusion.78
  139.2 1.5 fusion.78
  146.9 13.0 %while.72 = (s32[]{:T(128)}, f32[3,3,8,128]{3,2,1,0:T(8,128)S(1)}, f32[3,3,8,128]{3,2,1,0:T(8,128)S(1)}, f32[3,8,8]{2,1,0:T(8,128)S(1)}, f32[3,8,8,128]{3,1,2,0:...) while((s32[]{:T(128)}, f32[3,3,8,128]{3,2,1,0:T(8,128)S(1)}, ...), condition=%wide.region_6.6_spmd, body=%wide.region_1.5_spmd.sunk | while | flops 34108420 | bytes 7377393 | solution.py:98
  149.7 1.5 fusion.78
  154.0 1.5 fusion.78
  158.3 1.5 fusion.78
  166.1 13.0 %while.72 = (s32[]{:T(128)}, f32[3,3,8,128]{3,2,1,0:T(8,128)S(1)}, f32[3,3,8,128]{3,2,1,0:T(8,128)S(1)}, f32[3,8,8]{2,1,0:T(8,128)S(1)}, f32[3,8,8,128]{3,1,2,0:...) while((s32[]{:T(128)}, f32[3,3,8,128]{3,2,1,0:T(8,128)S(1)}, ...), condition=%wide.region_6.6_spmd, body=%wide.region_1.5_spmd.sunk | while | flops 34108420 | bytes 7377393 | solution.py:98
  168.9 1.5 fusion.78
  173.2 1.5 fusion.78
  177.5 1.5 fusion.78
  185.2 13.0 %while.72 = (s32[]{:T(128)}, f32[3,3,8,128]{3,2,1,0:T(8,128)S(1)}, f32[3,3,8,128]{3,2,1,0:T(8,128)S(1)}, f32[3,8,8]{2,1,0:T(8,128)S(1)}, f32[3,8,8,128]{3,1,2,0:...) while((s32[]{:T(128)}, f32[3,3,8,128]{3,2,1,0:T(8,128)S(1)}, ...), condition=%wide.region_6.6_spmd, body=%wide.region_1.5_spmd.sunk | while | flops 34108420 | bytes 7377393 | solution.py:98
  188.0 1.5 fusion.78
  192.4 1.5 fusion.78
  196.7 1.5 fusion.78
  204.4 13.0 %while.72 = (s32[]{:T(128)}, f32[3,3,8,128]{3,2,1,0:T(8,128)S(1)}, f32[3,3,8,128]{3,2,1,0:T(8,128)S(1)}, f32[3,8,8]{2,1,0:T(8,128)S(1)}, f32[3,8,8,128]{3,1,2,0:...) while((s32[]{:T(128)}, f32[3,3,8,128]{3,2,1,0:T(8,128)S(1)}, ...), condition=%wide.region_6.6_spmd, body=%wide.region_1.5_spmd.sunk | while | flops 34108420 | bytes 7377393 | solution.py:98
  207.2 1.5 fusion.78
  211.6 1.5 fusion.78
  215.9 1.5 fusion.78
  223.6 13.0 %while.72 = (s32[]{:T(128)}, f32[3,3,8,128]{3,2,1,0:T(8,128)S(1)}, f32[3,3,8,128]{3,2,1,0:T(8,128)S(1)}, f32[3,8,8]{2,1,0:T(8,128)S(1)}, f32[3,8,8,128]{3,1,2,0:...) while((s32[]{:T(128)}, f32[3,3,8,128]{3,2,1,0:T(8,128)S(1)}, ...), condition=%wide.region_6.6_spmd, body=%wide.region_1.5_spmd.sunk | while | flops 34108420 | bytes 7377393 | solution.py:98
  226.4 1.5 fusion.78
  230.7 1.5 fusion.78
  235.1 1.5 fusion.78
  242.8 13.0 %while.72 = (s32[]{:T(128)}, f32[3,3,8,128]{3,2,1,0:T(8,128)S(1)}, f32[3,3,8,128]{3,2,1,0:T(8,128)S(1)}, f32[3,8,8]{2,1,0:T(8,128)S(1)}, f32[3,8,8,128]{3,1,2,0:...) while((s32[]{:T(128)}, f32[3,3,8,128]{3,2,1,0:T(8,128)S(1)}, ...), condition=%wide.region_6.6_spmd, body=%wide.region_1.5_spmd.sunk | while | flops 34108420 | bytes 7377393 | solution.py:98
  245.6 1.5 fusion.78
  249.9 1.5 fusion.78
  254.3 1.5 fusion.78
  262.0 13.0 %while.72 = (s32[]{:T(128)}, f32[3,3,8,128]{3,2,1,0:T(8,128)S(1)}, f32[3,3,8,128]{3,2,1,0:T(8,128)S(1)}, f32[3,8,8]{2,1,0:T(8,128)S(1)}, f32[3,8,8,128]{3,1,2,0:...) while((s32[]{:T(128)}, f32[3,3,8,128]{3,2,1,0:T(8,128)S(1)}, ...), condition=%wide.region_6.6_spmd, body=%wide.region_1.5_spmd.sunk | while | flops 34108420 | bytes 7377393 | solution.py:98
  264.8 1.5 fusion.78
  269.1 1.5 fusion.78
  273.4 1.5 fusion.78
  275.5 5.3 %psum.35 = f32[8,8]{1,0:T(8,128)S(1)} all-reduce(f32[8,8]{1,0:T(8,128)S(1)} %bitcast_add_fusion.2), channel_id=1, replica_groups=mesh['xy_0'=2,'xy_1'=8,'xy_2'=2,'gz_0'=2,'gz_1'=4] {'xy_0'}, use_global_device_ids=true, to_apply=%region_15.16 | all-reduce | flops 64 | bytes 512 | tf_op jit(solution)/shard_map/psum | solution.py:47
  280.8 18.3 %psum.36 = f32[8,8]{1,0:T(8,128)S(1)} all-reduce(f32[8,8]{1,0:T(8,128)S(1)} %psum.35), channel_id=1, replica_groups=mesh['xy_0'=2,'xy_1'=8,'xy_2'=2,'gz_0'=2,'gz_1'=4] {'xy_1'}, use_global_device_ids=true, to_apply=%region_16.17 | all-reduce | flops 64 | bytes 512 | tf_op jit(solution)/shard_map/psum | solution.py:47
  299.1 4.1 %psum.37 = f32[8,8]{1,0:T(8,128)S(1)} all-reduce(f32[8,8]{1,0:T(8,128)S(1)} %psum.36), channel_id=1, replica_groups=mesh['xy_0'=2,'xy_1'=8,'xy_2'=2,'gz_0'=2,'gz_1'=4] {'xy_2'}, use_global_device_ids=true, to_apply=%region_17.18 | all-reduce | flops 64 | bytes 512 | tf_op jit(solution)/shard_map/psum | solution.py:47
  303.3 3.8 %psum.38 = f32[8,8]{1,0:T(8,128)S(1)} all-reduce(f32[8,8]{1,0:T(8,128)S(1)} %psum.37), channel_id=1, replica_groups=mesh['xy_0'=2,'xy_1'=8,'xy_2'=2,'gz_0'=2,'gz_1'=4] {'gz_0'}, use_global_device_ids=true, to_apply=%region_18.19 | all-reduce | flops 64 | bytes 512 | tf_op jit(solution)/shard_map/psum | solution.py:47
  307.0 9.5 %psum.39 = f32[8,8]{1,0:T(8,128)S(1)} all-reduce(f32[8,8]{1,0:T(8,128)S(1)} %psum.38), channel_id=1, replica_groups=mesh['xy_0'=2,'xy_1'=8,'xy_2'=2,'gz_0'=2,'gz_1'=4] {'gz_1'}, use_global_device_ids=true, to_apply=%region_19.20 | all-reduce | flops 64 | bytes 512 | tf_op jit(solution)/shard_map/psum | solution.py:47
  317.3 3.6 %collective-permute-start.5 = (f32[3,1,6,1,128]{4,3,2,1,0:T(1,128)S(1)}, f32[3,1,6,1,128]{4,3,2,1,0:T(1,128)S(1)}, u32[]{:S(2)}, u32[]{:S(2)}) collective-permute-start(f32[3,1,6,1,128]{4,3,2,1,0:T(1,128)S(1)} %get-tuple-element.419), channel_id=1, source_target_pairs={{1,0},{2,1},{3,2},{4,3},{5,4},{6,5},{7,6},{0,7},{9,8},{10,9},{11,1... | collective-permute-start | bytes 27656 | tf_op jit(solution)/shard_map/ppermute | solution.py:43
  (865 shorter events, 144.1 us)
Async XLA Ops:
  0.6 7.8 %copy-start.3 = (s32[1,6,4]{1,2,0:T(4,128)S(1)}, s32[1,6,4]{1,2,0:T(4,128)}, u32[]{:S(2)}) copy-start(s32[1,6,4]{1,2,0:T(4,128)} %param.27) | copy-start | bytes 292
  0.6 8.1 %copy-start.1 = (f32[3,1,6,4,128]{4,3,2,1,0:T(4,128)S(1)}, f32[3,1,6,4,128]{4,3,2,1,0:T(4,128)}, u32[]{:S(2)}) copy-start(f32[3,1,6,4,128]{4,3,2,1,0:T(4,128)} %param.24) | copy-start | bytes 110596
  0.7 8.1 %copy-start = (f32[3,1,6,4,128]{4,3,2,1,0:T(4,128)S(1)}, f32[3,1,6,4,128]{4,3,2,1,0:T(4,128)}, u32[]{:S(2)}) copy-start(f32[3,1,6,4,128]{4,3,2,1,0:T(4,128)} %param.25) | copy-start | bytes 110596
  0.7 7.9 %copy-start.2 = (f32[8,8]{1,0:T(8,128)S(1)}, f32[8,8]{1,0:T(8,128)}, u32[]{:S(2)}) copy-start(f32[8,8]{1,0:T(8,128)} %param.28) | copy-start | bytes 772
  3.9 5.6 %collective-permute-start = (f32[8,1,6,1,128]{4,0,3,2,1:T(8,128)S(1)}, f32[8,1,6,1,128]{4,0,3,2,1:T(8,128)S(1)}, u32[]{:S(2)}, u32[]{:S(2)}) collective-permute-start(f32[8,1,6,1,128]{4,0,3,2,1:T(8,128)S(1)} %get-tuple-element.417), channel_id=1, source_target_pairs={{0,1},{1,2},{2,3},{3,4},{4,5},{5,6},{6,7},{7,0},{8,9},{9,10},{10,1... | collective-permute-start | bytes 73736 | tf_op jit(solution)/shard_map/ppermute | solution.py:32
  6.0 3.5 %collective-permute-start.1 = (f32[8,1,6,1,128]{4,0,3,2,1:T(8,128)S(1)}, f32[8,1,6,1,128]{4,0,3,2,1:T(8,128)S(1)}, u32[]{:S(2)}, u32[]{:S(2)}) collective-permute-start(f32[8,1,6,1,128]{4,0,3,2,1:T(8,128)S(1)} %get-tuple-element.418), channel_id=1, source_target_pairs={{1,0},{2,1},{3,2},{4,3},{5,4},{6,5},{7,6},{0,7},{9,8},{10,9},{11,1... | collective-permute-start | bytes 73736 | tf_op jit(solution)/shard_map/ppermute | solution.py:35
  9.6 16.2 %collective-permute-start.2 = (f32[8,1,6,6,128]{4,0,3,2,1:T(8,128)S(1)}, f32[8,1,6,6,128]{4,0,3,2,1:T(8,128)S(1)}, u32[]{:S(2)}, u32[]{:S(2)}) collective-permute-start(f32[8,1,6,6,128]{4,0,3,2,1:T(8,128)S(1)} %pad_maximum_fusion.12), channel_id=1, source_target_pairs={{8,0},{16,8},{24,16},{32,24},{40,32},{48,40},{56,48},{64,56},{72,6... | collective-permute-start | bytes 442376 | tf_op jit(solution)/shard_map/ppermute | solution.py:43
  275.4 41.1 %collective-permute-start.3 = (f32[3,1,6,6,128]{4,3,2,1,0:T(8,128)S(1)}, f32[3,1,6,6,128]{4,3,2,1,0:T(8,128)S(1)}, u32[]{:S(2)}, u32[]{:S(2)}) collective-permute-start(f32[3,1,6,6,128]{4,3,2,1,0:T(8,128)S(1)} %slice.313), channel_id=1, source_target_pairs={{248,0},{0,8},{8,16},{16,24},{24,32},{32,40},{40,48},{48,56},{56,6... | collective-permute-start | bytes 165896 | tf_op jit(solution)/shard_map/ppermute | solution.py:43
  316.6 4.7 %collective-permute-start.4 = (f32[3,1,6,1,128]{4,3,2,1,0:T(1,128)S(1)}, f32[3,1,6,1,128]{4,3,2,1,0:T(1,128)S(1)}, u32[]{:S(2)}, u32[]{:S(2)}) collective-permute-start(f32[3,1,6,1,128]{4,3,2,1,0:T(1,128)S(1)} %get-tuple-element.420), channel_id=1, source_target_pairs={{7,0},{0,1},{1,2},{2,3},{3,4},{4,5},{5,6},{6,7},{15,8},{8,9},{9,10... | collective-permute-start | bytes 27656 | tf_op jit(solution)/shard_map/ppermute | solution.py:43
  317.3 4.4 %collective-permute-start.5 = (f32[3,1,6,1,128]{4,3,2,1,0:T(1,128)S(1)}, f32[3,1,6,1,128]{4,3,2,1,0:T(1,128)S(1)}, u32[]{:S(2)}, u32[]{:S(2)}) collective-permute-start(f32[3,1,6,1,128]{4,3,2,1,0:T(1,128)S(1)} %get-tuple-element.419), channel_id=1, source_target_pairs={{1,0},{2,1},{3,2},{4,3},{5,4},{6,5},{7,6},{0,7},{9,8},{10,9},{11,1... | collective-permute-start | bytes 27656 | tf_op jit(solution)/shard_map/ppermute | solution.py:43
where the time goes:
time: 329 us; the launch traced here: 322 us
  other arithmetic  132 us (40%)
  loops' own time  64.4 us (20%)
  matrix products  53.6 us (16%)
  blocking collectives  41 us (12%)
  local copies, waits for them, and re-layouts  17.2 us (5%)
  starting transfers between devices  12 us (4%)
    another operation x1, loops' own time, sweep(): lax.scan(advance, initial, jnp.asarray(shifts))  59.4 us
    reduce_sum x39, other arithmetic, pair_block(): away_part = -jnp.sum(response, axis=2)  58.7 us
    reduce_sum x42, other arithmetic, pair_block(): square = jnp.sum(displace * displace, axis=0)  44.8 us
    psum x5, blocking collectives, over_axes(): return functools.reduce(lax.psum, axes, array)  41 us
    dot_general x42, matrix products, pair_block(): jnp.einsum('sma,smb->mab', kind_home, mixed_row, precision=HIGHEST)  25.6 us
    dot_general x42, matrix products, pair_block(): weighted = jnp.einsum('sma,mab->smb', kind_home, weight, precision=HIGHEST)  16.8 us
    convert_element_type x13, other arithmetic, advance(): shift.astype(jnp.float32)  9.1 us
    slice x13, local copies, waits for them, and re-layouts, advance(): start = (0, home_start + shift[0], 1 + shift[1], 1 + shift[2], 0)  8.66 us
  transfers between devices with their start and end apart: 6, of which 3 were waited for; matrix products, arithmetic and copies ran while one was open for 4% of the time, Pallas kernels for 0%

commit v1 on v0

v1 whole, which is shorter than its diff:
```python
import math

import jax
import jax.numpy as jnp
from jax import lax
from jax.experimental import pallas as pl
from jax.experimental.pallas import tpu as pltpu
from jax.sharding import Mesh
from jax.sharding import PartitionSpec as P

AXES = ("y_hi", "z_ax", "core", "y_lo", "x_ax")
ROW = ("y_lo", "x_ax")
COL = ("y_hi", "z_ax", "core")
NX, NZ = 32, 8
step_size = 0.05
FAR = 1.0e4
NY = 6
ZC = 4
SLOTS = 128
KINDS = 8
FEATS = 112
HOMES = NY * ZC
bf16 = jnp.bfloat16
f32 = jnp.float32


def sublane(shape=(8, SLOTS)):
    return lax.broadcasted_iota(jnp.int32, shape, 0)


def pieces(v):
    high = v.astype(bf16).astype(f32)
    rest = v - high
    mid = rest.astype(bf16).astype(f32)
    return high, mid, rest - mid


def pick(row, lo, hi, value, other):
    return jnp.where((row >= lo) & (row < hi), value, other)


def row_sum(row, lo, hi, value):
    return jnp.sum(pick(row, lo, hi, value, 0.0), axis=0, keepdims=True)


def framed(raw, row, sx, sy, sz):
    shift = jnp.where(row == 0, sx, jnp.where(row == 1, sy, jnp.where(row == 2, sz, 0.0)))
    return raw + shift.astype(f32)


def bead_terms(raw, row, shifts):
    v = framed(raw, row, *shifts)
    back = pltpu.roll(v, 3, 0)
    square = row_sum(row, 0, 3, v * v)
    cross = row_sum(row, 3, 6, v * back)
    return v, back, square, cross


def far_features(raw, shifts, lhs_ref, feat_ref, slot):
    row = sublane()
    v, back, square, cross = bead_terms(raw, row, shifts)
    code = raw[6:7]
    ahead = pltpu.roll(v, 5, 0)
    gain = jnp.where(code < 0.0, -FAR, 1.0 - square)
    a = pick(row, 0, 3, ahead, pick(row, 3, 6, back, 0.0))
    ah, am, al = pieces(a)
    qh, qm, ql = pieces(gain)
    rh, rm, rl = pieces(cross)
    one = jnp.where(row == 6, 1.0, 0.0)
    last = row == 7
    lhs = jnp.concatenate(
        [
            jnp.where(last, qh, ah + one),
            jnp.where(last, qm, ah + one),
            jnp.where(last, ql, ah + one),
            jnp.where(last, rh, am),
            jnp.where(last, rm, am),
            jnp.where(last, rl, al),
            jnp.zeros((SLOTS - 48, SLOTS), f32),
        ],
        axis=0,
    )
    lhs_ref[slot] = lhs.T.astype(bf16)
    mask = code == row.astype(f32)
    high = v.astype(bf16).astype(f32)
    low = v - high
    rows = [jnp.where(mask, 1.0, 0.0)]
    for part, start in ((high, 0), (low, 0), (high, 3), (low, 3)):
        for k in range(3):
            rows.append(jnp.where(mask, part[start + k : start + k + 1], 0.0))
    rows.append(jnp.zeros((8, SLOTS), f32))
    feat_ref[slot] = jnp.concatenate(rows, axis=0).astype(bf16)


def home_features(raw, shifts, gram_ref, frame_ref, h):
    row = sublane()
    v, back, square, cross = bead_terms(raw, row, shifts)
    square = jnp.where(raw[6:7] < 0.0, FAR, square)
    u = pick(row, 3, 6, 2.0 * back, jnp.where(row == 6, -square, 0.0))
    p = pick(row, 0, 6, -v, jnp.where(row == 6, cross, 0.0))
    last = jnp.where(row == 7, 1.0, 0.0)
    uh, um, ul = pieces(u)
    ph, pm, pl_ = pieces(p)
    gram_ref[h, :, 0:SLOTS] = jnp.concatenate(
        [uh + last, um + last, ul + last, uh, um, uh], axis=0
    ).astype(bf16)
    gram_ref[h, :, SLOTS : 2 * SLOTS] = jnp.concatenate(
        [ph, pm, pl_, ph + last, pm + last, ph + last], axis=0
    ).astype(bf16)
    frame_ref[h] = jnp.where(row == 7, cross, v)


def pair_body(steps, last, group, home_ref, far_refs, table_ref, before_ref, matrix_before_ref,
              out_ref, matrix_ref, gram_ref, frame_ref, lhs_ref, feat_ref, acc_ref,
              moment_ref, kind_ref):
    count = len(steps)
    for i, sx in enumerate(steps):
        @pl.loop(0, 48)
        def _(n, i=i, sx=sx):
            z = n // 8
            ye = n % 8
            y = lax.rem(ye + 5, 6)
            far_features(
                far_refs[i][z, y],
                (sx - 0.5, (ye - 4).astype(f32), (z - 3).astype(f32)),
                lhs_ref, feat_ref, i * 48 + n,
            )

    @pl.loop(0, HOMES)
    def _(h):
        z = h // 6
        y = h % 6
        home_features(
            home_ref[z, y], (-0.5, (y - 3).astype(f32), (z - 2).astype(f32)),
            gram_ref, frame_ref, h,
        )

    @pl.loop(0, HOMES // group)
    def _(q):
        for j in range(group):
            h = q * group + j
            z = h // 6
            y = h % 6
            gram = gram_ref[h]
            acc = None
            for i in range(count):
                base = (i * 6 + z) * 8 + y
                for dz in range(3):
                    for dy in range(3):
                        slot = base + dz * 8 + dy
                        g = jnp.dot(lhs_ref[slot, :, 0:48], gram, preferred_element_type=f32)
                        e = jnp.maximum(g[:, :SLOTS], 0.0)
                        both = jnp.concatenate([e * e, e * g[:, SLOTS:]], axis=1)
                        high = both.astype(bf16)
                        low = (both - high.astype(f32)).astype(bf16)
                        feat = feat_ref[slot]
                        part = jnp.dot(
                            jnp.concatenate([feat, feat], axis=1),
                            jnp.concatenate([high, low], axis=0),
                            preferred_element_type=f32,
                        )
                        acc = part if acc is None else acc + part
            acc_ref[h] = acc

    table = table_ref[...]

    @pl.loop(0, HOMES)
    def _(h):
        z = h // 6
        y = h % 6
        v = frame_ref[h]
        code = v[6:7]
        mix = jnp.zeros((8, SLOTS), f32)
        for s in range(KINDS):
            mix = jnp.where(code == float(s), table[:, s : s + 1], mix)

        def part(f, half):
            return acc_ref[h, 8 * f : 8 * f + 8, half * SLOTS : (half + 1) * SLOTS]

        def mixed(value):
            return jnp.sum(value * mix, axis=0, keepdims=True)

        c1 = mixed(part(0, 0))
        c2 = mixed(part(0, 1))
        moment = v[7:8] * part(0, 0)
        rows = []
        for k in range(3):
            moment = moment - v[3 + k : 4 + k] * (part(1 + k, 0) + part(4 + k, 0))
            stretch = v[3 + k : 4 + k] * c1 - mixed(part(7 + k, 0) + part(10 + k, 0))
            bend = v[k : k + 1] * c2 - mixed(part(1 + k, 1) + part(4 + k, 1))
            rows.append(step_size * (6.0 * stretch - 24.0 * bend))
        moment_ref[h] = moment
        kind_ref[h] = jnp.where(code == sublane().astype(f32), 1.0, 0.0)
        if last:
            for k in range(3):
                out_ref[k, 0, y, pl.ds(z, 1), :] = rows[k] + before_ref[z, y, k : k + 1]
        else:
            for k in range(3):
                out_ref[z, y, k : k + 1] = rows[k] + v[3 + k : 4 + k]

    total = jnp.zeros((8, 8), f32)
    moments = jnp.concatenate([moment_ref[h] for h in range(HOMES)], axis=1)
    kinds = jnp.concatenate([kind_ref[h] for h in range(HOMES)], axis=1).astype(bf16)
    for piece in pieces(moments):
        total = total + lax.dot_general(
            piece.astype(bf16), kinds, (((1,), (1,)), ((), ())), preferred_element_type=f32
        )
    if last:
        total = total + matrix_before_ref[...]
    matrix_ref[...] = total


def pair_call(steps, last, group, home, fars, table, before, matrix_before):
    count = len(steps)
    vmem = pl.BlockSpec(memory_space=pltpu.VMEM)

    def body(home_ref, *refs):
        far_refs = refs[:count]
        table_ref = refs[count]
        rest = refs[count + 1 :]
        if last:
            before_ref, matrix_before_ref = rest[:2]
            rest = rest[2:]
        else:
            before_ref = matrix_before_ref = None
        pair_body(steps, last, group, home_ref, far_refs, table_ref, before_ref,
                  matrix_before_ref, *rest)

    out = (
        jax.ShapeDtypeStruct((3, 1, NY, ZC, SLOTS), f32)
        if last
        else jax.ShapeDtypeStruct((ZC, NY, 8, SLOTS), f32)
    )
    operands = [home, *fars, table]
    if last:
        operands += [before, matrix_before]
    return pl.pallas_call(
        body,
        out_shape=(out, jax.ShapeDtypeStruct((8, 8), f32)),
        in_specs=[vmem] * len(operands),
        out_specs=(vmem, vmem),
        scratch_shapes=[
            pltpu.VMEM((HOMES, 48, 2 * SLOTS), bf16),
            pltpu.VMEM((HOMES, 8, SLOTS), f32),
            pltpu.VMEM((48 * count, SLOTS, SLOTS), bf16),
            pltpu.VMEM((48 * count, FEATS, SLOTS), bf16),
            pltpu.VMEM((HOMES, FEATS, 2 * SLOTS), f32),
            pltpu.VMEM((HOMES, 8, SLOTS), f32),
            pltpu.VMEM((HOMES, 8, SLOTS), f32),
        ],
        compiler_params=pltpu.CompilerParams(vmem_limit_bytes=48 * 2**20),
        name="pairs_last" if last else "pairs_first",
    )(*operands)


def pack_body(counts_ref, pos_ref, cot_ref, species_ref, out_ref, low_ref, high_ref):
    lane = lax.broadcasted_iota(jnp.int32, (1, SLOTS), 1)
    for y in range(NY):
        for z in range(ZC):
            rows = [pos_ref[k, 0, y, z : z + 1, :] for k in range(3)]
            rows += [cot_ref[k, 0, y, z : z + 1, :] for k in range(3)]
            kind = jnp.where(lane < counts_ref[0, y, z], species_ref[0, y, z : z + 1, :], -1)
            rows += [kind.astype(f32), jnp.zeros((1, SLOTS), f32)]
            packed = jnp.concatenate(rows, axis=0)
            out_ref[z, y] = packed
            if z == 0:
                low_ref[0, y] = packed
            if z == ZC - 1:
                high_ref[0, y] = packed


def pack(counts, positions, cotangent, species):
    vmem = pl.BlockSpec(memory_space=pltpu.VMEM)
    return pl.pallas_call(
        pack_body,
        out_shape=(
            jax.ShapeDtypeStruct((ZC, NY, 8, SLOTS), f32),
            jax.ShapeDtypeStruct((1, NY, 8, SLOTS), f32),
            jax.ShapeDtypeStruct((1, NY, 8, SLOTS), f32),
        ),
        in_specs=[pl.BlockSpec(memory_space=pltpu.SMEM)] + [vmem] * 3,
        out_specs=(vmem,) * 3,
        name="pack",
    )(counts, positions, cotangent, species)


def move(block, dx, dz):
    pairs = []
    for i in range(NX):
        for j in range(NZ):
            pairs.append((i * NZ + j, (i + dx) % NX * NZ + (j + dz) % NZ))
    return lax.ppermute(block, AXES, pairs)


def summed(matrix):
    for group in (("core", "y_lo", "x_ax"), ("y_hi", "z_ax")):
        n = lax.axis_size(group)
        sent = jnp.broadcast_to(matrix[None], (n,) + matrix.shape)
        matrix = jnp.sum(lax.all_to_all(sent, group, 0, 0), axis=0)
    return matrix


def per_device(positions, cotangent, species, counts, amplitude):
    table = 0.5 * (amplitude + amplitude.T)
    home, low, high = pack(counts, positions, cotangent, species)
    below = move(high, 0, 1)
    above = move(low, 0, -1)
    column = jnp.concatenate([below, home, above], axis=0)
    left = move(column, 1, 0)
    right = move(column, -1, 0)
    part, matrix_part = pair_call((0.0,), False, 3, home, (column,), table, None, None)
    out, matrix = pair_call(
        (-1.0, 1.0), True, 2, home, (left, right), table, part, matrix_part
    )
    cells_total = NX * NY * NZ * ZC
    total = 6.0 * summed(matrix + matrix.T)
    return out, step_size * total / (2.0 * math.sqrt(cells_total / SLOTS))


def solution(mesh):
    finer = Mesh(mesh.devices.reshape(2, 8, 2, 2, 4), AXES)
    in_specs = (
        P(None, COL, None, ROW, None),
        P(None, COL, None, ROW, None),
        P(COL, None, ROW, None),
        P(COL, None, ROW),
        P(),
    )
    return jax.shard_map(
        per_device,
        mesh=finer,
        in_specs=in_specs,
        out_specs=(P(None, COL, None, ROW, None), P()),
        check_vma=False,
    )
```

time: 329 us -> 102 us (0.31); the launches traced: 322 us -> 102 us
  other arithmetic: 132 us -> 0.65 us
  loops' own time: 64.4 us -> 0 us
  Pallas kernels: 0 us -> 57.6 us
  matrix products: 53.6 us -> 0 us
  local copies, waits for them, and re-layouts: 17.2 us -> 2.5 us
  blocking collectives: 41 us -> 30.7 us
  starting transfers between devices: 12 us -> 8.13 us
    reduce_sum x98 -> x2, other arithmetic: 108 us -> 0.04 us  [summed(): matrix = jnp.sum(lax.all_to_all(sent, group, 0, 0), axis=0)]
    another operation x15 -> x0, loops' own time: 64.4 us -> none  [the longest x1 59.4 us: sweep(): lax.scan(advance, initial, jnp.asarray(shifts))]
    pallas_call x0 -> x3, Pallas kernels: none -> 57.6 us  [the longest x2 56 us: pair_call(): pl.pallas_call(body, out_shape=(out, jax.ShapeDtypeStruct((8, 8), f32)),...]
    dot_general x168 -> x0, matrix products: 53.6 us -> none  [the longest x42 25.6 us: pair_block(): jnp.einsum('sma,smb->mab', kind_home, mixed_row, precision=HIGHEST)]
    psum x5 -> x0, blocking collectives: 41 us -> none  [over_axes(): return functools.reduce(lax.psum, axes, array)]
    all_to_all x0 -> x2, blocking collectives: none -> 30.7 us  [summed(): matrix = jnp.sum(lax.all_to_all(sent, group, 0, 0), axis=0)]
    mul x82 -> x1, other arithmetic: 11.4 us -> 0.01 us  [per_device(): table = 0.5 * (amplitude + amplitude.T)]
    slice x174 -> x0, local copies, waits for them, and re-layouts: 11.2 us -> none  [the longest x13 8.66 us: advance(): start = (0, home_start + shift[0], 1 + shift[1], 1 + shift[2], 0)]
  transfers between devices with their start and end apart: 6 -> 4, of which waited for: 3 -> 1; matrix products, arithmetic and copies ran while one was open for 4% -> 1% of each run, Pallas kernels for 0% -> 20%
where the time goes in v1:
time: 102 us
  Pallas kernels  57.6 us (56%)
  blocking collectives  30.7 us (30%)
  starting transfers between devices  8.13 us (8%)
  local copies, waits for them, and re-layouts  2.5 us (2%)
  waiting for transfers between devices  1.37 us (1%)
    pallas_call x2, Pallas kernels, pair_call(): pl.pallas_call(body, out_shape=(out, jax.ShapeDtypeStruct((8, 8), f32)),...  56 us
    all_to_all x2, blocking collectives, summed(): matrix = jnp.sum(lax.all_to_all(sent, group, 0, 0), axis=0)  30.7 us
    ppermute x4, starting transfers between devices, move(): return lax.ppermute(block, AXES, pairs)  8.13 us
    unnamed x8, local copies, waits for them, and re-layouts  2.4 us
  transfers between devices with their start and end apart: 4, of which 1 were waited for; matrix products, arithmetic and copies ran while one was open for 1% of the time, Pallas kernels for 20%

profile of v1, /device:TPU:1, one launch (start us, length us, event | category | flops | bytes accessed | tf_op | source)
XLA Modules:
  0.0 101.6 jit_solution(11629860087459464811)
XLA Ops:
  0.6 1.4 %copy.13.counts_ref = s32[1,6,4]{2,1,0:T(8,128)} copy(s32[1,6,4]{1,2,0:T(4,128)} %param.8) | data formatting | bytes 192 | tf_op args[3]
  2.0 0.0 copy-start.1
  2.0 1.5 %pack.1 = (f32[4,6,8,128]{3,2,1,0:T(8,128)}, f32[1,6,8,128]{3,2,1,0:T(8,128)}, f32[1,6,8,128]{3,2,1,0:T(8,128)}) custom-call(s32[1,6,4]{2,1,0:T(8,128)} %copy.13.counts_ref, f32[3,1,6,4,128]{4,3,2,1,0:T(4,128)} %pos_ref.1, f32[3,1,6,4,128]{4,3,2,1,0:T(4,128)} %cot_ref.1, s32[1,6,4,128]{3,2,1,0:T(4,128)} %species_ref.1), custom_call_target="tpu_custom_call" | custom-call | tf_op jit(solution)/shard_map/pack/pallas_call | solution.py:274
  3.5 2.0 %collective-permute-start = (f32[1,6,8,128]{3,2,1,0:T(8,128)}, f32[1,6,8,128]{3,2,1,0:T(8,128)S(1)}, u32[]{:S(2)}, u32[]{:S(2)}) collective-permute-start(f32[1,6,8,128]{3,2,1,0:T(8,128)} %get-tuple-element.10), channel_id=1, source_target_pairs={{0,1},{1,2},{2,3},{3,4},{4,5},{5,6},{6,7},{7,0},{8,9},{9,10},{10,1... | collective-permute-start | bytes 73736 | tf_op jit(solution)/shard_map/ppermute | solution.py:292
  5.6 2.3 %collective-permute-start.1 = (f32[1,6,8,128]{3,2,1,0:T(8,128)}, f32[1,6,8,128]{3,2,1,0:T(8,128)S(1)}, u32[]{:S(2)}, u32[]{:S(2)}) collective-permute-start(f32[1,6,8,128]{3,2,1,0:T(8,128)} %get-tuple-element.11), channel_id=1, source_target_pairs={{0,7},{1,0},{2,1},{3,2},{4,3},{5,4},{6,5},{7,6},{8,15},{9,8},{10,9... | collective-permute-start | bytes 73736 | tf_op jit(solution)/shard_map/ppermute | solution.py:292
  7.9 0.0 copy-done.1
  7.9 0.1 copy.14
  7.9 1.3 %collective-permute-done = f32[1,6,8,128]{3,2,1,0:T(8,128)S(1)} collective-permute-done((f32[1,6,8,128]{3,2,1,0:T(8,128)}, f32[1,6,8,128]{3,2,1,0:T(8,128)S(1)}, u32[]{:S(2)}, u32[]{:S(2)}) %collective-permute-start) | collective-permute-done | bytes 24608 | tf_op jit(solution)/shard_map/ppermute | solution.py:292
  9.3 0.0 copy-start
  9.3 1.0 constant_dynamic-update-slice_fusion.1
  10.3 0.0 collective-permute-done.1
  10.3 3.5 %collective-permute-start.2 = (f32[6,6,8,128]{3,2,1,0:T(8,128)S(1)}, f32[6,6,8,128]{3,2,1,0:T(8,128)S(1)}, u32[]{:S(2)}, u32[]{:S(2)}) collective-permute-start(f32[6,6,8,128]{3,2,1,0:T(8,128)S(1)} %constant_dynamic-update-slice_fusion.refs_0_), channel_id=1, source_target_pairs={{0,8},{1,9},{2,10},{3,11},{4,12},{5,13},{6,14},{7,15},{8,16},{9,17... | collective-permute-start | bytes 442376 | tf_op jit(solution)/shard_map/ppermute | solution.py:292
  13.8 0.3 collective-permute-start.3
  14.1 0.0 copy-done
  14.1 20.3 %pairs_first.1 = (f32[4,6,8,128]{3,2,1,0:T(8,128)S(1)}, f32[8,8]{1,0:T(8,128)S(1)}) custom-call(f32[4,6,8,128]{3,2,1,0:T(8,128)S(1)} %copy-done, f32[6,6,8,128]{3,2,1,0:T(8,128)S(1)} %constant_dynamic-update-slice_fusion.refs_0_, f32[8,8]{1,0:T(8,128)S(1)} %fusion.refs_1_.refs_2_), custom_call_target="tpu_custom_call" | custom-call | tf_op jit(solution)/shard_map/pairs_first/pallas_call | solution.py:237
  34.4 0.0 collective-permute-done.2.refs_0_
  34.4 0.0 collective-permute-done.3.refs_1_
  34.4 35.7 %pairs_last.1 = (f32[3,1,6,4,128]{4,3,2,1,0:T(4,128)}, f32[8,8]{1,0:T(8,128)S(1)}) custom-call(f32[4,6,8,128]{3,2,1,0:T(8,128)S(1)} %copy-done, f32[6,6,8,128]{3,2,1,0:T(8,128)S(1)} %collective-permute-done.2.refs_0_, f32[6,6,8,128]{3,2,1,0:T(8,128)S(1)} %collective-permute-done.3.refs_1_, f32[8,8]{1,0:T(8,128)S(1)} %fusion.refs_1_.refs_2_, ...), custom_call_target="tpu_custom_call" | custom-call | tf_op jit(solution)/shard_map/pairs_last/pallas_call | solution.py:237
  70.2 0.1 copy.15
  70.3 15.3 %all_to_all.10 = f32[16,8,8]{2,1,0:T(8,128)S(1)} all-to-all(f32[16,8,8]{2,1,0:T(8,128)S(1)} %broadcast_in_dim.4), channel_id=1, replica_groups=mesh['y_hi'=2,'z_ax'=8,'core'=2,'y_lo'=2,'x_ax'=4] {'core','y_lo','x_ax'}, dimensions={0} | all-to-all | bytes 8192 | tf_op jit(solution)/shard_map/all_to_all | solution.py:299
  85.6 15.5 %all_to_all.11 = f32[16,8,8]{2,1,0:T(8,128)S(1)} all-to-all(f32[16,8,8]{2,1,0:T(8,128)S(1)} %broadcast_in_dim.5), channel_id=1, replica_groups=mesh['y_hi'=2,'z_ax'=8,'core'=2,'y_lo'=2,'x_ax'=4] {'y_hi','z_ax'}, dimensions={0} | all-to-all | bytes 8192 | tf_op jit(solution)/shard_map/all_to_all | solution.py:299
  101.0 0.6 broadcast_multiply_fusion
  (8 shorter events, 0.1 us)
Async XLA Ops:
  2.0 5.9 %copy-start.1 = (f32[8,8]{1,0:T(8,128)S(1)}, f32[8,8]{1,0:T(8,128)}, u32[]{:S(2)}) copy-start(f32[8,8]{1,0:T(8,128)} %param.9) | copy-start | bytes 772
  3.5 5.7 %collective-permute-start = (f32[1,6,8,128]{3,2,1,0:T(8,128)}, f32[1,6,8,128]{3,2,1,0:T(8,128)S(1)}, u32[]{:S(2)}, u32[]{:S(2)}) collective-permute-start(f32[1,6,8,128]{3,2,1,0:T(8,128)} %get-tuple-element.10), channel_id=1, source_target_pairs={{0,1},{1,2},{2,3},{3,4},{4,5},{5,6},{6,7},{7,0},{8,9},{9,10},{10,1... | collective-permute-start | bytes 73736 | tf_op jit(solution)/shard_map/ppermute | solution.py:292
  5.6 4.7 %collective-permute-start.1 = (f32[1,6,8,128]{3,2,1,0:T(8,128)}, f32[1,6,8,128]{3,2,1,0:T(8,128)S(1)}, u32[]{:S(2)}, u32[]{:S(2)}) collective-permute-start(f32[1,6,8,128]{3,2,1,0:T(8,128)} %get-tuple-element.11), channel_id=1, source_target_pairs={{0,7},{1,0},{2,1},{3,2},{4,3},{5,4},{6,5},{7,6},{8,15},{9,8},{10,9... | collective-permute-start | bytes 73736 | tf_op jit(solution)/shard_map/ppermute | solution.py:292
  9.3 4.8 %copy-start = (f32[4,6,8,128]{3,2,1,0:T(8,128)S(1)}, f32[4,6,8,128]{3,2,1,0:T(8,128)}, u32[]{:S(2)}) copy-start(f32[4,6,8,128]{3,2,1,0:T(8,128)} %get-tuple-element.9.home_ref) | copy-start | bytes 294916
  10.3 24.1 %collective-permute-start.2 = (f32[6,6,8,128]{3,2,1,0:T(8,128)S(1)}, f32[6,6,8,128]{3,2,1,0:T(8,128)S(1)}, u32[]{:S(2)}, u32[]{:S(2)}) collective-permute-start(f32[6,6,8,128]{3,2,1,0:T(8,128)S(1)} %constant_dynamic-update-slice_fusion.refs_0_), channel_id=1, source_target_pairs={{0,8},{1,9},{2,10},{3,11},{4,12},{5,13},{6,14},{7,15},{8,16},{9,17... | collective-permute-start | bytes 442376 | tf_op jit(solution)/shard_map/ppermute | solution.py:292
  13.8 20.7 %collective-permute-start.3 = (f32[6,6,8,128]{3,2,1,0:T(8,128)S(1)}, f32[6,6,8,128]{3,2,1,0:T(8,128)S(1)}, u32[]{:S(2)}, u32[]{:S(2)}) collective-permute-start(f32[6,6,8,128]{3,2,1,0:T(8,128)S(1)} %constant_dynamic-update-slice_fusion.refs_0_), channel_id=1, source_target_pairs={{0,248},{1,249},{2,250},{3,251},{4,252},{5,253},{6,254},{7,255},{8... | collective-permute-start | bytes 442376 | tf_op jit(solution)/shard_map/ppermute | solution.py:292

commit v2 on v1

--- a/solution.py
+++ b/solution.py
@@ -115,7 +115,7 @@
               moment_ref, kind_ref):
     count = len(steps)
     for i, sx in enumerate(steps):
-        @pl.loop(0, 48)
+        @pl.loop(0, 48, unroll=4)
         def _(n, i=i, sx=sx):
             z = n // 8
             ye = n % 8
@@ -126,7 +126,7 @@
                 lhs_ref, feat_ref, i * 48 + n,
             )
 
-    @pl.loop(0, HOMES)
+    @pl.loop(0, HOMES, unroll=4)
     def _(h):
         z = h // 6
         y = h % 6
@@ -163,8 +163,9 @@
             acc_ref[h] = acc
 
     table = table_ref[...]
-
-    @pl.loop(0, HOMES)
+    columns = [jnp.broadcast_to(table[:, s : s + 1], (8, SLOTS)) for s in range(KINDS)]
+
+    @pl.loop(0, HOMES, unroll=4)
     def _(h):
         z = h // 6
         y = h % 6
@@ -172,7 +173,7 @@
         code = v[6:7]
         mix = jnp.zeros((8, SLOTS), f32)
         for s in range(KINDS):
-            mix = jnp.where(code == float(s), table[:, s : s + 1], mix)
+            mix = jnp.where(code == float(s), columns[s], mix)
 
         def part(f, half):
             return acc_ref[h, 8 * f : 8 * f + 8, half * SLOTS : (half + 1) * SLOTS]
@@ -293,11 +294,9 @@
 
 
 def summed(matrix):
-    for group in (("core", "y_lo", "x_ax"), ("y_hi", "z_ax")):
-        n = lax.axis_size(group)
-        sent = jnp.broadcast_to(matrix[None], (n,) + matrix.shape)
-        matrix = jnp.sum(lax.all_to_all(sent, group, 0, 0), axis=0)
-    return matrix
+    sent = jnp.broadcast_to(matrix.reshape(1, KINDS * KINDS), (NX * NZ, KINDS * KINDS))
+    heard = lax.all_to_all(sent, AXES, 0, 0, tiled=True)
+    return jnp.sum(heard, axis=0).reshape(KINDS, KINDS)
 
 
 def per_device(positions, cotangent, species, counts, amplitude):

time: 102 us -> 83.2 us (0.82)
  Pallas kernels: 57.6 us -> 41.5 us
  blocking collectives: 30.7 us -> 27.8 us
    pallas_call x2, Pallas kernels: 56 us -> 39.9 us  [pair_call(): pl.pallas_call(body, out_shape=(out, jax.ShapeDtypeStruct((8, 8), f32)),...]
    all_to_all x2 -> x1, blocking collectives: 30.7 us -> 27.8 us  [summed(): heard = lax.all_to_all(sent, AXES, 0, 0, tiled=True)]
  transfers between devices with their start and end apart: 4 -> 4, of which waited for: 1 -> 1; matrix products, arithmetic and copies ran while one was open for 1% -> 1% of each run, Pallas kernels for 20% -> 17%
where the time goes in v2:
time: 83.2 us; the launch traced here: 83 us
  Pallas kernels  41.5 us (50%)
  blocking collectives  27.8 us (33%)
  starting transfers between devices  8.13 us (10%)
  local copies, waits for them, and re-layouts  3.31 us (4%)
  waiting for transfers between devices  1.37 us (2%)
    pallas_call x2, Pallas kernels, pair_call(): pl.pallas_call(body, out_shape=(out, jax.ShapeDtypeStruct((8, 8), f32)),...  39.9 us
    all_to_all x1, blocking collectives, summed(): heard = lax.all_to_all(sent, AXES, 0, 0, tiled=True)  27.8 us
    ppermute x4, starting transfers between devices, move(): return lax.ppermute(block, AXES, pairs)  8.13 us
    unnamed x8, local copies, waits for them, and re-layouts  2.4 us
  transfers between devices with their start and end apart: 4, of which 1 were waited for; matrix products, arithmetic and copies ran while one was open for 1% of the time, Pallas kernels for 17%

profile of v2, /device:TPU:1, one launch (start us, length us, event | category | flops | bytes accessed | tf_op | source)
XLA Modules:
  0.0 83.0 jit_solution(3497084935375489594)
XLA Ops:
  0.6 1.4 %copy.13.counts_ref = s32[1,6,4]{2,1,0:T(8,128)} copy(s32[1,6,4]{1,2,0:T(4,128)} %param.8) | data formatting | bytes 192 | tf_op args[3]
  2.0 0.0 copy-start.1
  2.0 1.6 %pack.1 = (f32[4,6,8,128]{3,2,1,0:T(8,128)}, f32[1,6,8,128]{3,2,1,0:T(8,128)}, f32[1,6,8,128]{3,2,1,0:T(8,128)}) custom-call(s32[1,6,4]{2,1,0:T(8,128)} %copy.13.counts_ref, f32[3,1,6,4,128]{4,3,2,1,0:T(4,128)} %pos_ref.1, f32[3,1,6,4,128]{4,3,2,1,0:T(4,128)} %cot_ref.1, s32[1,6,4,128]{3,2,1,0:T(4,128)} %species_ref.1), custom_call_target="tpu_custom_call" | custom-call | tf_op jit(solution)/shard_map/pack/pallas_call | solution.py:275
  3.5 2.0 %collective-permute-start = (f32[1,6,8,128]{3,2,1,0:T(8,128)}, f32[1,6,8,128]{3,2,1,0:T(8,128)S(1)}, u32[]{:S(2)}, u32[]{:S(2)}) collective-permute-start(f32[1,6,8,128]{3,2,1,0:T(8,128)} %get-tuple-element.10), channel_id=1, source_target_pairs={{0,1},{1,2},{2,3},{3,4},{4,5},{5,6},{6,7},{7,0},{8,9},{9,10},{10,1... | collective-permute-start | bytes 73736 | tf_op jit(solution)/shard_map/ppermute | solution.py:293
  5.6 2.3 %collective-permute-start.1 = (f32[1,6,8,128]{3,2,1,0:T(8,128)}, f32[1,6,8,128]{3,2,1,0:T(8,128)S(1)}, u32[]{:S(2)}, u32[]{:S(2)}) collective-permute-start(f32[1,6,8,128]{3,2,1,0:T(8,128)} %get-tuple-element.11), channel_id=1, source_target_pairs={{0,7},{1,0},{2,1},{3,2},{4,3},{5,4},{6,5},{7,6},{8,15},{9,8},{10,9... | collective-permute-start | bytes 73736 | tf_op jit(solution)/shard_map/ppermute | solution.py:293
  7.9 0.0 copy-done.1
  7.9 0.1 copy.14
  7.9 1.3 %collective-permute-done = f32[1,6,8,128]{3,2,1,0:T(8,128)S(1)} collective-permute-done((f32[1,6,8,128]{3,2,1,0:T(8,128)}, f32[1,6,8,128]{3,2,1,0:T(8,128)S(1)}, u32[]{:S(2)}, u32[]{:S(2)}) %collective-permute-start) | collective-permute-done | bytes 24608 | tf_op jit(solution)/shard_map/ppermute | solution.py:293
  9.3 0.0 copy-start
  9.3 1.0 %constant_dynamic-update-slice_fusion.1 = f32[6,6,8,128]{3,2,1,0:T(8,128)S(1)} fusion(f32[6,6,8,128]{3,2,1,0:T(8,128)S(1)} %constant_dynamic-update-slice_fusion.2, f32[4,6,8,128]{3,2,1,0:T(8,128)} %get-tuple-element.9.home_ref), kind=kLoop, calls=%fused_computation.1 | loop fusion | bytes 196608
  10.3 0.0 collective-permute-done.1
  10.3 3.5 %collective-permute-start.2 = (f32[6,6,8,128]{3,2,1,0:T(8,128)S(1)}, f32[6,6,8,128]{3,2,1,0:T(8,128)S(1)}, u32[]{:S(2)}, u32[]{:S(2)}) collective-permute-start(f32[6,6,8,128]{3,2,1,0:T(8,128)S(1)} %constant_dynamic-update-slice_fusion.refs_0_), channel_id=1, source_target_pairs={{0,8},{1,9},{2,10},{3,11},{4,12},{5,13},{6,14},{7,15},{8,16},{9,17... | collective-permute-start | bytes 442376 | tf_op jit(solution)/shard_map/ppermute | solution.py:293
  13.8 0.3 collective-permute-start.3
  14.1 0.0 copy-done
  14.1 14.2 %pairs_first.1 = (f32[4,6,8,128]{3,2,1,0:T(8,128)S(1)}, f32[8,8]{1,0:T(8,128)S(1)}) custom-call(f32[4,6,8,128]{3,2,1,0:T(8,128)S(1)} %copy-done, f32[6,6,8,128]{3,2,1,0:T(8,128)S(1)} %constant_dynamic-update-slice_fusion.refs_0_, f32[8,8]{1,0:T(8,128)S(1)} %fusion.refs_1_.refs_2_), custom_call_target="tpu_custom_call" | custom-call | tf_op jit(solution)/shard_map/pairs_first/pallas_call | solution.py:238
  28.3 0.0 collective-permute-done.2.refs_0_
  28.3 0.0 collective-permute-done.3.refs_1_
  28.3 25.7 %pairs_last.1 = (f32[3,1,6,4,128]{4,3,2,1,0:T(4,128)}, f32[8,8]{1,0:T(8,128)S(1)}) custom-call(f32[4,6,8,128]{3,2,1,0:T(8,128)S(1)} %copy-done, f32[6,6,8,128]{3,2,1,0:T(8,128)S(1)} %collective-permute-done.2.refs_0_, f32[6,6,8,128]{3,2,1,0:T(8,128)S(1)} %collective-permute-done.3.refs_1_, f32[8,8]{1,0:T(8,128)S(1)} %fusion.refs_1_.refs_2_, ...), custom_call_target="tpu_custom_call" | custom-call | tf_op jit(solution)/shard_map/pairs_last/pallas_call | solution.py:238
  54.0 0.1 copy.15
  54.1 0.1 broadcast_in_dim.7
  54.2 0.1 broadcast_in_dim.8
  54.3 27.8 %all_to_all.6 = f32[256,1,64]{2,1,0:T(1,128)S(1)} all-to-all(f32[256,1,64]{2,1,0:T(1,128)S(1)} %broadcast_in_dim.8), channel_id=1, replica_groups=mesh['y_hi'=2,'z_ax'=8,'core'=2,'y_lo'=2,'x_ax'=4] {'y_hi','z_ax','core'..., dimensions={0} | all-to-all | bytes 131072 | tf_op jit(solution)/shard_map/all_to_all | solution.py:298
  82.0 0.3 reduce_sum.9
  82.3 0.7 div.10
  (5 shorter events, 0.0 us)
Async XLA Ops:
  2.0 5.9 %copy-start.1 = (f32[8,8]{1,0:T(8,128)S(1)}, f32[8,8]{1,0:T(8,128)}, u32[]{:S(2)}) copy-start(f32[8,8]{1,0:T(8,128)} %param.9) | copy-start | bytes 772
  3.5 5.7 %collective-permute-start = (f32[1,6,8,128]{3,2,1,0:T(8,128)}, f32[1,6,8,128]{3,2,1,0:T(8,128)S(1)}, u32[]{:S(2)}, u32[]{:S(2)}) collective-permute-start(f32[1,6,8,128]{3,2,1,0:T(8,128)} %get-tuple-element.10), channel_id=1, source_target_pairs={{0,1},{1,2},{2,3},{3,4},{4,5},{5,6},{6,7},{7,0},{8,9},{9,10},{10,1... | collective-permute-start | bytes 73736 | tf_op jit(solution)/shard_map/ppermute | solution.py:293
  5.6 4.7 %collective-permute-start.1 = (f32[1,6,8,128]{3,2,1,0:T(8,128)}, f32[1,6,8,128]{3,2,1,0:T(8,128)S(1)}, u32[]{:S(2)}, u32[]{:S(2)}) collective-permute-start(f32[1,6,8,128]{3,2,1,0:T(8,128)} %get-tuple-element.11), channel_id=1, source_target_pairs={{0,7},{1,0},{2,1},{3,2},{4,3},{5,4},{6,5},{7,6},{8,15},{9,8},{10,9... | collective-permute-start | bytes 73736 | tf_op jit(solution)/shard_map/ppermute | solution.py:293
  9.3 4.8 %copy-start = (f32[4,6,8,128]{3,2,1,0:T(8,128)S(1)}, f32[4,6,8,128]{3,2,1,0:T(8,128)}, u32[]{:S(2)}) copy-start(f32[4,6,8,128]{3,2,1,0:T(8,128)} %get-tuple-element.9.home_ref) | copy-start | bytes 294916
  10.3 18.0 %collective-permute-start.2 = (f32[6,6,8,128]{3,2,1,0:T(8,128)S(1)}, f32[6,6,8,128]{3,2,1,0:T(8,128)S(1)}, u32[]{:S(2)}, u32[]{:S(2)}) collective-permute-start(f32[6,6,8,128]{3,2,1,0:T(8,128)S(1)} %constant_dynamic-update-slice_fusion.refs_0_), channel_id=1, source_target_pairs={{0,8},{1,9},{2,10},{3,11},{4,12},{5,13},{6,14},{7,15},{8,16},{9,17... | collective-permute-start | bytes 442376 | tf_op jit(solution)/shard_map/ppermute | solution.py:293
  13.8 14.5 %collective-permute-start.3 = (f32[6,6,8,128]{3,2,1,0:T(8,128)S(1)}, f32[6,6,8,128]{3,2,1,0:T(8,128)S(1)}, u32[]{:S(2)}, u32[]{:S(2)}) collective-permute-start(f32[6,6,8,128]{3,2,1,0:T(8,128)S(1)} %constant_dynamic-update-slice_fusion.refs_0_), channel_id=1, source_target_pairs={{0,248},{1,249},{2,250},{3,251},{4,252},{5,253},{6,254},{7,255},{8... | collective-permute-start | bytes 442376 | tf_op jit(solution)/shard_map/ppermute | solution.py:293

commit v3 on v2

--- a/solution.py
+++ b/solution.py
@@ -18,7 +18,6 @@
 ZC = 4
 SLOTS = 128
 KINDS = 8
-FEATS = 112
 HOMES = NY * ZC
 bf16 = jnp.bfloat16
 f32 = jnp.float32
@@ -88,7 +87,10 @@
     for part, start in ((high, 0), (low, 0), (high, 3), (low, 3)):
         for k in range(3):
             rows.append(jnp.where(mask, part[start + k : start + k + 1], 0.0))
-    rows.append(jnp.zeros((8, SLOTS), f32))
+    if feat_ref.shape[1] == 128:
+        rows += [jnp.where(mask, r, 0.0) for r in (rh, rm, rl)]
+    else:
+        rows.append(jnp.zeros((8, SLOTS), f32))
     feat_ref[slot] = jnp.concatenate(rows, axis=0).astype(bf16)
 
 
@@ -110,10 +112,9 @@
     frame_ref[h] = jnp.where(row == 7, cross, v)
 
 
-def pair_body(steps, last, group, home_ref, far_refs, table_ref, before_ref, matrix_before_ref,
-              out_ref, matrix_ref, gram_ref, frame_ref, lhs_ref, feat_ref, acc_ref,
-              moment_ref, kind_ref):
-    count = len(steps)
+def pair_body(steps, tiles, group, stage, home_ref, far_refs, table_ref, before_ref,
+              matrix_before_ref, out_ref, matrix_ref, gram_ref, frame_ref, lhs_ref, feat_ref,
+              acc_ref, own_ref, moment_ref, kind_ref):
     for i, sx in enumerate(steps):
         @pl.loop(0, 48, unroll=4)
         def _(n, i=i, sx=sx):
@@ -143,23 +144,22 @@
             y = h % 6
             gram = gram_ref[h]
             acc = None
-            for i in range(count):
-                base = (i * 6 + z) * 8 + y
-                for dz in range(3):
-                    for dy in range(3):
-                        slot = base + dz * 8 + dy
-                        g = jnp.dot(lhs_ref[slot, :, 0:48], gram, preferred_element_type=f32)
-                        e = jnp.maximum(g[:, :SLOTS], 0.0)
-                        both = jnp.concatenate([e * e, e * g[:, SLOTS:]], axis=1)
-                        high = both.astype(bf16)
-                        low = (both - high.astype(f32)).astype(bf16)
-                        feat = feat_ref[slot]
-                        part = jnp.dot(
-                            jnp.concatenate([feat, feat], axis=1),
-                            jnp.concatenate([high, low], axis=0),
-                            preferred_element_type=f32,
-                        )
-                        acc = part if acc is None else acc + part
+            for i, dz, dy in tiles:
+                slot = (i * 6 + z + dz) * 8 + y + dy
+                g = jnp.dot(lhs_ref[slot, :, 0:48], gram, preferred_element_type=f32)
+                e = jnp.maximum(g[:, :SLOTS], 0.0)
+                both = jnp.concatenate([e * e, e * g[:, SLOTS:]], axis=1)
+                high = both.astype(bf16)
+                low = (both - high.astype(f32)).astype(bf16)
+                feat = feat_ref[slot]
+                part = jnp.dot(
+                    jnp.concatenate([feat, feat], axis=1),
+                    jnp.concatenate([high, low], axis=0),
+                    preferred_element_type=f32,
+                )
+                if stage == 0 and acc is None:
+                    own_ref[h] = part[56:, :SLOTS]
+                acc = part if acc is None else acc + part
             acc_ref[h] = acc
 
     table = table_ref[...]
@@ -181,76 +181,92 @@
         def mixed(value):
             return jnp.sum(value * mix, axis=0, keepdims=True)
 
+        def away(f):
+            if stage == 0:
+                return part(f, 0) - own_ref[h, 8 * f - 56 : 8 * f - 48]
+            return part(f, 0)
+
         c1 = mixed(part(0, 0))
         c2 = mixed(part(0, 1))
-        moment = v[7:8] * part(0, 0)
         rows = []
         for k in range(3):
-            moment = moment - v[3 + k : 4 + k] * (part(1 + k, 0) + part(4 + k, 0))
             stretch = v[3 + k : 4 + k] * c1 - mixed(part(7 + k, 0) + part(10 + k, 0))
             bend = v[k : k + 1] * c2 - mixed(part(1 + k, 1) + part(4 + k, 1))
             rows.append(step_size * (6.0 * stretch - 24.0 * bend))
-        moment_ref[h] = moment
-        kind_ref[h] = jnp.where(code == sublane().astype(f32), 1.0, 0.0)
-        if last:
+        if stage < 2:
+            moment = v[7:8] * part(0, 0) + (away(13) + away(14) + away(15))
             for k in range(3):
+                moment = moment - v[3 + k : 4 + k] * (part(1 + k, 0) + part(4 + k, 0))
+                moment = moment - v[k : k + 1] * (away(7 + k) + away(10 + k))
+            moment_ref[h] = moment
+            kind_ref[h] = jnp.where(code == sublane().astype(f32), 1.0, 0.0)
+        for k in range(3):
+            if stage == 2:
                 out_ref[k, 0, y, pl.ds(z, 1), :] = rows[k] + before_ref[z, y, k : k + 1]
-        else:
-            for k in range(3):
-                out_ref[z, y, k : k + 1] = rows[k] + v[3 + k : 4 + k]
-
-    total = jnp.zeros((8, 8), f32)
-    moments = jnp.concatenate([moment_ref[h] for h in range(HOMES)], axis=1)
-    kinds = jnp.concatenate([kind_ref[h] for h in range(HOMES)], axis=1).astype(bf16)
-    for piece in pieces(moments):
-        total = total + lax.dot_general(
-            piece.astype(bf16), kinds, (((1,), (1,)), ((), ())), preferred_element_type=f32
-        )
-    if last:
-        total = total + matrix_before_ref[...]
-    matrix_ref[...] = total
-
-
-def pair_call(steps, last, group, home, fars, table, before, matrix_before):
+            else:
+                old = v[3 + k : 4 + k] if stage == 0 else before_ref[z, y, k : k + 1]
+                out_ref[z, y, k : k + 1] = rows[k] + old
+
+    if stage < 2:
+        total = jnp.zeros((8, 8), f32)
+        moments = jnp.concatenate([moment_ref[h] for h in range(HOMES)], axis=1)
+        kinds = jnp.concatenate([kind_ref[h] for h in range(HOMES)], axis=1).astype(bf16)
+        for piece in pieces(moments):
+            total = total + lax.dot_general(
+                piece.astype(bf16), kinds, (((1,), (1,)), ((), ())), preferred_element_type=f32
+            )
+        if stage == 1:
+            total = total + matrix_before_ref[...]
+        matrix_ref[...] = total
+
+
+def pair_call(steps, tiles, group, stage, home, fars, table, before=None, matrix_before=None):
     count = len(steps)
+    feats = 112 if stage == 2 else 128
     vmem = pl.BlockSpec(memory_space=pltpu.VMEM)
+    operands = [home, *fars, table]
+    if stage > 0:
+        operands.append(before)
+    if stage == 1:
+        operands.append(matrix_before)
+    scratch = [
+        pltpu.VMEM((HOMES, 48, 2 * SLOTS), bf16),
+        pltpu.VMEM((HOMES, 8, SLOTS), f32),
+        pltpu.VMEM((48 * count, SLOTS, SLOTS), bf16),
+        pltpu.VMEM((48 * count, feats, SLOTS), bf16),
+        pltpu.VMEM((HOMES, feats, 2 * SLOTS), f32),
+    ]
+    if stage < 2:
+        scratch += [pltpu.VMEM((HOMES, 72, SLOTS), f32)] + [pltpu.VMEM((HOMES, 8, SLOTS), f32)] * 2
 
     def body(home_ref, *refs):
         far_refs = refs[:count]
         table_ref = refs[count]
-        rest = refs[count + 1 :]
-        if last:
-            before_ref, matrix_before_ref = rest[:2]
-            rest = rest[2:]
-        else:
-            before_ref = matrix_before_ref = None
-        pair_body(steps, last, group, home_ref, far_refs, table_ref, before_ref,
-                  matrix_before_ref, *rest)
-
-    out = (
-        jax.ShapeDtypeStruct((3, 1, NY, ZC, SLOTS), f32)
-        if last
-        else jax.ShapeDtypeStruct((ZC, NY, 8, SLOTS), f32)
-    )
-    operands = [home, *fars, table]
-    if last:
-        operands += [before, matrix_before]
+        refs = list(refs[count + 1 :])
+        before_ref = refs.pop(0) if stage > 0 else None
+        matrix_before_ref = refs.pop(0) if stage == 1 else None
+        out_ref = refs.pop(0)
+        matrix_ref = refs.pop(0) if stage < 2 else None
+        if stage == 2:
+            refs += [None] * 3
+        pair_body(steps, tiles, group, stage, home_ref, far_refs, table_ref, before_ref,
+                  matrix_before_ref, out_ref, matrix_ref, *refs)
+
+    if stage == 2:
+        out = (jax.ShapeDtypeStruct((3, 1, NY, ZC, SLOTS), f32),)
+    else:
+        out = (
+            jax.ShapeDtypeStruct((ZC, NY, 8, SLOTS), f32),
+            jax.ShapeDtypeStruct((8, 8), f32),
+        )
     return pl.pallas_call(
         body,
-        out_shape=(out, jax.ShapeDtypeStruct((8, 8), f32)),
+        out_shape=out,
         in_specs=[vmem] * len(operands),
-        out_specs=(vmem, vmem),
-        scratch_shapes=[
-            pltpu.VMEM((HOMES, 48, 2 * SLOTS), bf16),
-            pltpu.VMEM((HOMES, 8, SLOTS), f32),
-            pltpu.VMEM((48 * count, SLOTS, SLOTS), bf16),
-            pltpu.VMEM((48 * count, FEATS, SLOTS), bf16),
-            pltpu.VMEM((HOMES, FEATS, 2 * SLOTS), f32),
-            pltpu.VMEM((HOMES, 8, SLOTS), f32),
-            pltpu.VMEM((HOMES, 8, SLOTS), f32),
-        ],
+        out_specs=(vmem,) * len(out),
+        scratch_shapes=scratch,
         compiler_params=pltpu.CompilerParams(vmem_limit_bytes=48 * 2**20),
-        name="pairs_last" if last else "pairs_first",
+        name=("pairs_own", "pairs_left", "pairs_rest")[stage],
     )(*operands)
 
 
@@ -293,10 +309,12 @@
     return lax.ppermute(block, AXES, pairs)
 
 
-def summed(matrix):
-    sent = jnp.broadcast_to(matrix.reshape(1, KINDS * KINDS), (NX * NZ, KINDS * KINDS))
-    heard = lax.all_to_all(sent, AXES, 0, 0, tiled=True)
-    return jnp.sum(heard, axis=0).reshape(KINDS, KINDS)
+OWN_HALF = [(0, 1, 1), (0, 1, 2), (0, 2, 0), (0, 2, 1), (0, 2, 2)]
+OWN_OTHER = [(0, 1, 0), (0, 0, 0), (0, 0, 1), (0, 0, 2)]
+
+
+def whole(i):
+    return [(i, dz, dy) for dz in range(3) for dy in range(3)]
 
 
 def per_device(positions, cotangent, species, counts, amplitude):
@@ -307,12 +325,18 @@
     column = jnp.concatenate([below, home, above], axis=0)
     left = move(column, 1, 0)
     right = move(column, -1, 0)
-    part, matrix_part = pair_call((0.0,), False, 3, home, (column,), table, None, None)
-    out, matrix = pair_call(
-        (-1.0, 1.0), True, 2, home, (left, right), table, part, matrix_part
+    part, matrix = pair_call((0.0,), OWN_HALF, 4, 0, home, (column,), table)
+    part, matrix = pair_call((-1.0,), whole(0), 3, 1, home, (left,), table, part, matrix)
+    sent = jnp.broadcast_to(matrix.reshape(1, KINDS * KINDS), (NX * NZ, KINDS * KINDS))
+    sent, part = lax.optimization_barrier((sent, part))
+    heard = lax.all_to_all(sent, AXES, 0, 0, tiled=True)
+    (out,) = pair_call(
+        (0.0, 1.0), OWN_OTHER + whole(1), 2, 2, home, (column, right), table, part
     )
+    heard, out = lax.optimization_barrier((heard, out))
+    matrix = jnp.sum(heard, axis=0).reshape(KINDS, KINDS)
     cells_total = NX * NY * NZ * ZC
-    total = 6.0 * summed(matrix + matrix.T)
+    total = 6.0 * (matrix + matrix.T)
     return out, step_size * total / (2.0 * math.sqrt(cells_total / SLOTS))
 
 

time: 83.2 us -> 75.8 us (0.911)
  blocking collectives: 27.8 us -> 0 us
  starting transfers between devices: 8.13 us -> 23.3 us
  Pallas kernels: 41.5 us -> 46.3 us
    all_to_all x1 -> x0, blocking collectives: 27.8 us -> none  [summed(): heard = lax.all_to_all(sent, AXES, 0, 0, tiled=True)]
    all_to_all x0 -> x1, starting transfers between devices: none -> 15.1 us  [per_device(): heard = lax.all_to_all(sent, AXES, 0, 0, tiled=True)]
    pallas_call x2 -> x3, Pallas kernels: 39.9 us -> 44.7 us  [pair_call(): pl.pallas_call(body, out_shape=out, in_specs=[vmem] * len(operands), out_...]
  transfers between devices with their start and end apart: 4 -> 5, of which waited for: 1 -> 1; matrix products, arithmetic and copies ran while one was open for 1% -> 2% of each run, Pallas kernels for 17% -> 59%
where the time goes in v3:
time: 75.8 us; the launch traced here: 75.6 us
  Pallas kernels  46.3 us (61%)
  starting transfers between devices  23.3 us (31%)
  local copies, waits for them, and re-layouts  3.32 us (4%)
  waiting for transfers between devices  1.36 us (2%)
    pallas_call x3, Pallas kernels, pair_call(): pl.pallas_call(body, out_shape=out, in_specs=[vmem] * len(operands), out_...  44.7 us
    all_to_all x1, starting transfers between devices, per_device(): heard = lax.all_to_all(sent, AXES, 0, 0, tiled=True)  15.1 us
    ppermute x4, starting transfers between devices, move(): return lax.ppermute(block, AXES, pairs)  8.13 us
    unnamed x8, local copies, waits for them, and re-layouts  2.4 us
    pallas_call x1, Pallas kernels, pack(): pl.pallas_call(pack_body, out_shape=(jax.ShapeDtypeStruct((ZC, NY, 8, SLO...  1.56 us
  transfers between devices with their start and end apart: 5, of which 1 were waited for; matrix products, arithmetic and copies ran while one was open for 2% of the time, Pallas kernels for 59%

profile of v3, /device:TPU:1, one launch (start us, length us, event | category | flops | bytes accessed | tf_op | source)
XLA Modules:
  0.0 75.6 jit_solution(6020614925274891286)
XLA Ops:
  0.6 1.4 %copy.10.counts_ref = s32[1,6,4]{2,1,0:T(8,128)} copy(s32[1,6,4]{1,2,0:T(4,128)} %param.8) | data formatting | bytes 192 | tf_op args[3]
  2.0 0.0 copy-start.1
  2.0 1.6 %pack.1 = (f32[4,6,8,128]{3,2,1,0:T(8,128)}, f32[1,6,8,128]{3,2,1,0:T(8,128)}, f32[1,6,8,128]{3,2,1,0:T(8,128)}) custom-call(s32[1,6,4]{2,1,0:T(8,128)} %copy.10.counts_ref, f32[3,1,6,4,128]{4,3,2,1,0:T(4,128)} %pos_ref.1, f32[3,1,6,4,128]{4,3,2,1,0:T(4,128)} %cot_ref.1, s32[1,6,4,128]{3,2,1,0:T(4,128)} %species_ref.1), custom_call_target="tpu_custom_call" | custom-call | tf_op jit(solution)/shard_map/pack/pallas_call | solution.py:291
  3.5 2.0 %collective-permute-start = (f32[1,6,8,128]{3,2,1,0:T(8,128)}, f32[1,6,8,128]{3,2,1,0:T(8,128)S(1)}, u32[]{:S(2)}, u32[]{:S(2)}) collective-permute-start(f32[1,6,8,128]{3,2,1,0:T(8,128)} %get-tuple-element.14), channel_id=1, source_target_pairs={{0,1},{1,2},{2,3},{3,4},{4,5},{5,6},{6,7},{7,0},{8,9},{9,10},{10,1... | collective-permute-start | bytes 73736 | tf_op jit(solution)/shard_map/ppermute | solution.py:309
  5.6 2.3 %collective-permute-start.1 = (f32[1,6,8,128]{3,2,1,0:T(8,128)}, f32[1,6,8,128]{3,2,1,0:T(8,128)S(1)}, u32[]{:S(2)}, u32[]{:S(2)}) collective-permute-start(f32[1,6,8,128]{3,2,1,0:T(8,128)} %get-tuple-element.15), channel_id=1, source_target_pairs={{0,7},{1,0},{2,1},{3,2},{4,3},{5,4},{6,5},{7,6},{8,15},{9,8},{10,9... | collective-permute-start | bytes 73736 | tf_op jit(solution)/shard_map/ppermute | solution.py:309
  7.9 0.0 copy-done.1
  7.9 0.1 copy.11
  7.9 1.3 %collective-permute-done = f32[1,6,8,128]{3,2,1,0:T(8,128)S(1)} collective-permute-done((f32[1,6,8,128]{3,2,1,0:T(8,128)}, f32[1,6,8,128]{3,2,1,0:T(8,128)S(1)}, u32[]{:S(2)}, u32[]{:S(2)}) %collective-permute-start) | collective-permute-done | bytes 24608 | tf_op jit(solution)/shard_map/ppermute | solution.py:309
  9.3 0.0 copy-start
  9.3 1.0 %constant_dynamic-update-slice_fusion.1 = f32[6,6,8,128]{3,2,1,0:T(8,128)S(1)} fusion(f32[6,6,8,128]{3,2,1,0:T(8,128)S(1)} %constant_dynamic-update-slice_fusion.2, f32[4,6,8,128]{3,2,1,0:T(8,128)} %get-tuple-element.13.home_ref), kind=kLoop, calls=%fused_computation.1 | loop fusion | bytes 196608
  10.3 0.0 collective-permute-done.1
  10.3 3.5 %collective-permute-start.2 = (f32[6,6,8,128]{3,2,1,0:T(8,128)S(1)}, f32[6,6,8,128]{3,2,1,0:T(8,128)S(1)}, u32[]{:S(2)}, u32[]{:S(2)}) collective-permute-start(f32[6,6,8,128]{3,2,1,0:T(8,128)S(1)} %constant_dynamic-update-slice_fusion.refs_0_), channel_id=1, source_target_pairs={{0,8},{1,9},{2,10},{3,11},{4,12},{5,13},{6,14},{7,15},{8,16},{9,17... | collective-permute-start | bytes 442376 | tf_op jit(solution)/shard_map/ppermute | solution.py:309
  13.8 0.3 collective-permute-start.3
  14.1 0.0 copy-done
  14.1 8.9 %pairs_own.1 = (f32[4,6,8,128]{3,2,1,0:T(8,128)S(1)}, f32[8,8]{1,0:T(8,128)S(1)}) custom-call(f32[4,6,8,128]{3,2,1,0:T(8,128)S(1)} %copy-done, f32[6,6,8,128]{3,2,1,0:T(8,128)S(1)} %constant_dynamic-update-slice_fusion.refs_0_, f32[8,8]{1,0:T(8,128)S(1)} %fusion.1.refs_1_.refs_2_), custom_call_target="tpu_custom_call" | custom-call | tf_op jit(solution)/shard_map/pairs_own/pallas_call | solution.py:262
  23.0 0.0 collective-permute-done.2.refs_0_
  23.0 14.3 %pairs_left.1 = (f32[4,6,8,128]{3,2,1,0:T(8,128)S(1)}, f32[8,8]{1,0:T(8,128)S(1)}) custom-call(f32[4,6,8,128]{3,2,1,0:T(8,128)S(1)} %copy-done, f32[6,6,8,128]{3,2,1,0:T(8,128)S(1)} %collective-permute-done.2.refs_0_, f32[8,8]{1,0:T(8,128)S(1)} %fusion.1.refs_1_.refs_2_, f32[4,6,8,128]{3,2,1,0:T(8,128)S(1)} %get-tuple-element.16.refs_2_, ...), custom_call_target="tpu_custom_call" | custom-call | tf_op jit(solution)/shard_map/pairs_left/pallas_call | solution.py:262
  37.3 0.1 broadcast_in_dim.7
  37.4 0.7 broadcast_in_dim.8
  38.0 15.1 %all-to-all-start = ((f32[256,1,64]{2,1,0:T(1,128)}), f32[256,1,64]{2,1,0:T(1,128)S(1)}, u32[]{:S(2)}, u32[]{:S(2)}) async-start(f32[256,1,64]{2,1,0:T(1,128)} %bitcast.1), calls=%async_computation | async-start | bytes 262144 | tf_op jit(solution)/shard_map/all_to_all | solution.py:332
  53.2 0.0 collective-permute-done.3.refs_1_
  53.2 21.6 %pairs_rest.1 = f32[3,1,6,4,128]{4,3,2,1,0:T(4,128)} custom-call(f32[4,6,8,128]{3,2,1,0:T(8,128)S(1)} %copy-done, f32[6,6,8,128]{3,2,1,0:T(8,128)S(1)} %constant_dynamic-update-slice_fusion.refs_0_, f32[6,6,8,128]{3,2,1,0:T(8,128)S(1)} %collective-permute-done.3.refs_1_, f32[8,8]{1,0:T(8,128)S(1)} %fusion.1.refs_1_.refs_2_, ...), custom_call_target="tpu_custom_call" | custom-call | tf_op jit(solution)/shard_map/pairs_rest/pallas_call | solution.py:262
  74.8 0.0 all-to-all-done
  74.8 0.1 reduce_sum.9
  74.8 0.1 reshape.11
  74.9 0.1 copy.12
  75.0 0.6 fusion
  (3 shorter events, 0.0 us)
Async XLA Ops:
  2.0 5.9 %copy-start.1 = (f32[8,8]{1,0:T(8,128)S(1)}, f32[8,8]{1,0:T(8,128)}, u32[]{:S(2)}) copy-start(f32[8,8]{1,0:T(8,128)} %param.9) | copy-start | bytes 772
  3.5 5.7 %collective-permute-start = (f32[1,6,8,128]{3,2,1,0:T(8,128)}, f32[1,6,8,128]{3,2,1,0:T(8,128)S(1)}, u32[]{:S(2)}, u32[]{:S(2)}) collective-permute-start(f32[1,6,8,128]{3,2,1,0:T(8,128)} %get-tuple-element.14), channel_id=1, source_target_pairs={{0,1},{1,2},{2,3},{3,4},{4,5},{5,6},{6,7},{7,0},{8,9},{9,10},{10,1... | collective-permute-start | bytes 73736 | tf_op jit(solution)/shard_map/ppermute | solution.py:309
  5.6 4.7 %collective-permute-start.1 = (f32[1,6,8,128]{3,2,1,0:T(8,128)}, f32[1,6,8,128]{3,2,1,0:T(8,128)S(1)}, u32[]{:S(2)}, u32[]{:S(2)}) collective-permute-start(f32[1,6,8,128]{3,2,1,0:T(8,128)} %get-tuple-element.15), channel_id=1, source_target_pairs={{0,7},{1,0},{2,1},{3,2},{4,3},{5,4},{6,5},{7,6},{8,15},{9,8},{10,9... | collective-permute-start | bytes 73736 | tf_op jit(solution)/shard_map/ppermute | solution.py:309
  9.3 4.8 %copy-start = (f32[4,6,8,128]{3,2,1,0:T(8,128)S(1)}, f32[4,6,8,128]{3,2,1,0:T(8,128)}, u32[]{:S(2)}) copy-start(f32[4,6,8,128]{3,2,1,0:T(8,128)} %get-tuple-element.13.home_ref) | copy-start | bytes 294916
  10.3 12.7 %collective-permute-start.2 = (f32[6,6,8,128]{3,2,1,0:T(8,128)S(1)}, f32[6,6,8,128]{3,2,1,0:T(8,128)S(1)}, u32[]{:S(2)}, u32[]{:S(2)}) collective-permute-start(f32[6,6,8,128]{3,2,1,0:T(8,128)S(1)} %constant_dynamic-update-slice_fusion.refs_0_), channel_id=1, source_target_pairs={{0,8},{1,9},{2,10},{3,11},{4,12},{5,13},{6,14},{7,15},{8,16},{9,17... | collective-permute-start | bytes 442376 | tf_op jit(solution)/shard_map/ppermute | solution.py:309
  13.8 39.4 %collective-permute-start.3 = (f32[6,6,8,128]{3,2,1,0:T(8,128)S(1)}, f32[6,6,8,128]{3,2,1,0:T(8,128)S(1)}, u32[]{:S(2)}, u32[]{:S(2)}) collective-permute-start(f32[6,6,8,128]{3,2,1,0:T(8,128)S(1)} %constant_dynamic-update-slice_fusion.refs_0_), channel_id=1, source_target_pairs={{0,248},{1,249},{2,250},{3,251},{4,252},{5,253},{6,254},{7,255},{8... | collective-permute-start | bytes 442376 | tf_op jit(solution)/shard_map/ppermute | solution.py:309
  38.0 36.7 %all-to-all-start = ((f32[256,1,64]{2,1,0:T(1,128)}), f32[256,1,64]{2,1,0:T(1,128)S(1)}, u32[]{:S(2)}, u32[]{:S(2)}) async-start(f32[256,1,64]{2,1,0:T(1,128)} %bitcast.1), calls=%async_computation | async-start | bytes 262144 | tf_op jit(solution)/shard_map/all_to_all | solution.py:332
